TPU v7x, 512 devices: a whole 4x4x16 slice. The times are simulated.
512 devices in a mesh: side: 2 (over y_hi), dp: 16 (over y_lo, x, core), grp: 16 (over z).
Axes of the slice: x: 4, y: 4 (y_hi: 2, y_lo: 2; y = y_hi * 2 + y_lo), z: 16, core: 2. Of those that a mesh axis runs over, the one named last changes fastest.
Arguments:
- attn_inputs: bfloat16 [2, 2, 32768, 2048], P('side', None, ('dp', 'grp')), may hold values from -120 to 120
- token_weight: float32 [32768], P(('dp', 'grp')), may hold values from 0.05 to 37.5
- enc_lens: int32 [16, 8], P('dp'), may hold values from 1 to 5, 16 in all within a row
- dec_lens: int32 [16, 8], P('dp'), may hold values from 1 to 5, 16 in all within a row
Outputs:
- attn_results: bfloat16 [2, 2, 32768, 2048], P('side', None, ('dp', 'grp'))
Inputs may be any that keep to these rules, and one draw needn't show every extreme that they name: `enc_lens`: row p lists, in pack order, how many blocks of 128 tokens the encoder part of each of pack p's 8 sequences takes; each row sums to 16 and its largest entry is exactly 5. `dec_lens`: row p lists the decoder blocks of the same 8 sequences in the same order; each row sums to 16 and its largest entry is exactly 5.
All inputs are finite; a program needn't handle non-finite values.
Results may differ from a plain program's by a relative error of at most 0.02.
Values may be sent and summed in bfloat16 or wider, within the bound.
No kernel may reach another device: no remote copies, remote signals or barrier semaphores. Data moves between devices by JAX's collectives and lax.ppermute only.
A program may use at most 64 MiB of HBM per device.

v0:
```python
import math

import jax
import jax.numpy as jnp
from jax import lax
from jax.sharding import Mesh
from jax.sharding import PartitionSpec as P

HD = 64
BLOCK = 128
DP_GRP = ("dp_0", "dp_1", "dp_2", "grp")
DP = ("dp_0", "dp_1", "dp_2")


def over_axes(value, axes):
    for axis in axes:
        value = lax.psum(value, axis)
    return value


def partner_2(block, axis, stride):
    count = lax.axis_size(axis)
    route = []
    for low in range(count):
        high = low | 1 << stride
        if high != low and high < count:
            route += [(low, high), (high, low)]
    return lax.ppermute(block, axis, route)


def segment_of(blocks, block_ends):
    return jnp.sum((blocks[..., None] >= block_ends).astype(jnp.int32), axis=-1)


def windows(row_lens, col_lens, block_count, window_blocks):
    row_ends = jnp.cumsum(row_lens)
    col_ends = jnp.cumsum(col_lens)
    col_starts = col_ends - col_lens
    blocks = jnp.arange(block_count, dtype=jnp.int32)
    row_seg = segment_of(blocks, row_ends)
    seq_count = col_starts.shape[0]
    matched = row_seg[:, None] == jnp.arange(seq_count, dtype=jnp.int32)[None, :]
    first_block = jnp.sum(jnp.where(matched, col_starts[None, :], 0), axis=1)
    first_block = jnp.minimum(first_block, block_count - window_blocks)
    picks = first_block[:, None] + jnp.arange(window_blocks, dtype=jnp.int32)[None, :]
    allowed = segment_of(picks, col_ends) == row_seg[:, None]
    return (picks, allowed)


def query_pass(queries, cotangent, keys_in, values_in, picks, allowed, with_grad):
    block_count = queries.shape[0] // BLOCK
    feature_count = queries.shape[1]
    head_count = feature_count // HD
    window_rows = picks.shape[1] * BLOCK
    score_scale = 1.0 / math.sqrt(HD)
    query_blocks = queries.reshape(block_count, BLOCK, head_count, HD)
    cot_blocks = cotangent.reshape(block_count, BLOCK, head_count, HD)
    key_blocks = keys_in.reshape(block_count, BLOCK, feature_count)
    value_blocks = values_in.reshape(block_count, BLOCK, feature_count)

    def query_one_group(group_index):
        first_block = group_index * 4
        query_now = lax.dynamic_slice_in_dim(query_blocks, first_block, 4, 0)
        cot_now = lax.dynamic_slice_in_dim(cot_blocks, first_block, 4, 0)
        picked = lax.dynamic_slice_in_dim(picks, first_block, 4, 0).reshape(-1)
        allowed_now = lax.dynamic_slice_in_dim(allowed, first_block, 4, 0)
        key_window = jnp.take(key_blocks, picked, axis=0).reshape(4, window_rows, head_count, HD)
        value_window = jnp.take(value_blocks, picked, axis=0).reshape(
            4, window_rows, head_count, HD
        )
        key_mask = jnp.repeat(allowed_now, BLOCK, axis=1)[:, None, None, :]
        scores = (
            jnp.einsum("gqhd,gkhd->ghqk", query_now, key_window, preferred_element_type=jnp.float32)
            * score_scale
        )
        scores = jnp.where(key_mask, scores, -jnp.inf)
        row_max = jnp.max(scores, axis=-1, keepdims=True)
        log_total = row_max + jnp.log(jnp.sum(jnp.exp(scores - row_max), axis=-1, keepdims=True))
        probs = jnp.exp(scores - log_total)
        probs_b = probs.astype(jnp.bfloat16)
        attended = jnp.einsum(
            "ghqk,gkhd->gqhd", probs_b, value_window, preferred_element_type=jnp.float32
        ).astype(jnp.bfloat16)
        row_dot = jnp.transpose(
            jnp.sum(cot_now.astype(jnp.float32) * attended.astype(jnp.float32), axis=-1), (0, 2, 1)
        )
        if with_grad:
            dprobs = jnp.einsum(
                "gqhd,gkhd->ghqk", cot_now, value_window, preferred_element_type=jnp.float32
            )
            dscores = (probs * (dprobs - row_dot[..., None]) * score_scale).astype(jnp.bfloat16)
            query_grad = jnp.einsum(
                "ghqk,gkhd->gqhd", dscores, key_window, preferred_element_type=jnp.float32
            ).astype(jnp.bfloat16)
        else:
            query_grad = attended
        return (attended, query_grad, log_total[..., 0], row_dot)

    attended, query_grad, log_total, row_dot = lax.map(
        query_one_group, jnp.arange(block_count // 4, dtype=jnp.int32)
    )
    attended = attended.reshape(block_count * BLOCK, feature_count)
    query_grad = query_grad.reshape(block_count * BLOCK, feature_count)
    log_total = log_total.reshape(block_count, head_count, BLOCK)
    row_dot = row_dot.reshape(block_count, head_count, BLOCK)
    return (attended, query_grad, log_total, row_dot)


def key_pass(queries, cotangent, keys_in, values_in, log_total, row_dot, picks, allowed):
    block_count = queries.shape[0] // BLOCK
    feature_count = queries.shape[1]
    head_count = feature_count // HD
    window_blocks = picks.shape[1]
    window_rows = window_blocks * BLOCK
    score_scale = 1.0 / math.sqrt(HD)
    query_blocks = queries.reshape(block_count, BLOCK, feature_count)
    cot_blocks = cotangent.reshape(block_count, BLOCK, feature_count)
    key_blocks = keys_in.reshape(block_count, BLOCK, head_count, HD)
    value_blocks = values_in.reshape(block_count, BLOCK, head_count, HD)

    def key_one_group(group_index):
        first_block = group_index * 4
        key_now = lax.dynamic_slice_in_dim(key_blocks, first_block, 4, 0)
        value_now = lax.dynamic_slice_in_dim(value_blocks, first_block, 4, 0)
        picked = lax.dynamic_slice_in_dim(picks, first_block, 4, 0).reshape(-1)
        allowed_now = lax.dynamic_slice_in_dim(allowed, first_block, 4, 0)
        query_window = jnp.take(query_blocks, picked, axis=0).reshape(
            4, window_rows, head_count, HD
        )
        cot_window = jnp.take(cot_blocks, picked, axis=0).reshape(4, window_rows, head_count, HD)
        total_window = jnp.take(log_total, picked, axis=0).reshape(
            4, window_blocks, head_count, BLOCK
        )
        total_window = jnp.transpose(total_window, (0, 2, 1, 3)).reshape(4, head_count, window_rows)
        dot_window = jnp.take(row_dot, picked, axis=0).reshape(4, window_blocks, head_count, BLOCK)
        dot_window = jnp.transpose(dot_window, (0, 2, 1, 3)).reshape(4, head_count, window_rows)
        query_mask = jnp.repeat(allowed_now, BLOCK, axis=1)[:, None, :, None]
        scores = (
            jnp.einsum("gqhd,gkhd->ghqk", query_window, key_now, preferred_element_type=jnp.float32)
            * score_scale
        )
        scores = jnp.where(query_mask, scores, -jnp.inf)
        probs = jnp.exp(scores - total_window[..., None])
        probs_b = probs.astype(jnp.bfloat16)
        value_grad = jnp.einsum(
            "ghqk,gqhd->gkhd", probs_b, cot_window, preferred_element_type=jnp.float32
        ).astype(jnp.bfloat16)
        dprobs = jnp.einsum(
            "gqhd,gkhd->ghqk", cot_window, value_now, preferred_element_type=jnp.float32
        )
        dscores = (probs * (dprobs - dot_window[..., None]) * score_scale).astype(jnp.bfloat16)
        key_grad = jnp.einsum(
            "ghqk,gqhd->gkhd", dscores, query_window, preferred_element_type=jnp.float32
        ).astype(jnp.bfloat16)
        return (key_grad, value_grad)

    key_grad, value_grad = lax.map(key_one_group, jnp.arange(block_count // 4, dtype=jnp.int32))
    return (
        key_grad.reshape(block_count * BLOCK, feature_count),
        value_grad.reshape(block_count * BLOCK, feature_count),
    )


def per_device(attn_inputs, token_weight, enc_lens, dec_lens):
    local_rows = attn_inputs[0]
    row_count = local_rows.shape[1]
    is_decoder = lax.axis_index("side") == 1
    weight_sum = over_axes(jnp.sum(token_weight), DP_GRP)
    factor = row_count * lax.axis_size(DP) * lax.axis_size("grp") / weight_sum
    scaled = (local_rows[1].astype(jnp.float32) * (token_weight * factor)[:, None]).astype(
        jnp.bfloat16
    )
    second_slot = jnp.where(is_decoder, scaled, local_rows[1])
    prepared = jnp.stack([local_rows[0], second_slot])
    heads_in = lax.all_to_all(prepared, "grp", split_axis=2, concat_axis=1, tiled=True)
    block_count = heads_in.shape[1] // BLOCK
    window_blocks = min(5, block_count // 2 + 1)
    enc_row = enc_lens[0]
    dec_row = dec_lens[0]
    dec_picks, dec_allowed = windows(dec_row, enc_row, block_count, window_blocks)
    enc_picks, enc_allowed = windows(enc_row, dec_row, block_count, window_blocks)
    partner = partner_2(heads_in, "side", 0)

    def decoder_work():
        attended, query_grad, log_total, row_dot = query_pass(
            heads_in[0], heads_in[1], partner[0], partner[1], dec_picks, dec_allowed, True
        )
        return jnp.stack([attended, query_grad])

    def encoder_work():
        attended, unused_grad, log_total, row_dot = query_pass(
            partner[0], partner[1], heads_in[0], heads_in[1], dec_picks, dec_allowed, False
        )
        key_grad, value_grad = key_pass(
            partner[0],
            partner[1],
            heads_in[0],
            heads_in[1],
            log_total,
            row_dot,
            enc_picks,
            enc_allowed,
        )
        return jnp.stack([key_grad, value_grad])

    final = lax.cond(is_decoder, decoder_work, encoder_work)
    result_rows = lax.all_to_all(final, "grp", split_axis=1, concat_axis=2, tiled=True)
    return result_rows[None]


def solution(mesh):
    torus = Mesh(
        mesh.devices.reshape(mesh.shape["side"], 2, 4, 2, mesh.shape["grp"]),
        ("side", "dp_0", "dp_1", "dp_2", "grp"),
    )
    placed = (P("side", None, DP_GRP, None), P(DP_GRP), P(DP, None), P(DP, None))
    return jax.shard_map(
        per_device,
        mesh=torus,
        in_specs=placed,
        out_specs=P("side", None, DP_GRP, None),
        check_vma=False,
    )
```

profile of v0, /device:TPU:8, one launch (start us, length us, event | category | flops | bytes accessed | tf_op | source)
XLA Modules:
  0.0 377.1 jit_solution(8199865065601751451)
XLA Ops:
  1.3 9.3 %psum.28 = f32[]{:T(128)} all-reduce(f32[]{:T(128)} %reduce_sum.100), channel_id=1, replica_groups=mesh['side'=2,'dp_0'=2,'dp_1'=4,'dp_2'=2,'grp'=16] {'dp_0'}, use_global_device_ids=true, to_apply=%region_1.0 | all-reduce | flops 1 | bytes 8 | tf_op jit(solution)/shard_map/psum | solution.py:17
  10.6 8.3 %psum.29 = f32[]{:T(128)} all-reduce(f32[]{:T(128)} %psum.28), channel_id=1, replica_groups=mesh['side'=2,'dp_0'=2,'dp_1'=4,'dp_2'=2,'grp'=16] {'dp_1'}, use_global_device_ids=true, to_apply=%region_2.0 | all-reduce | flops 1 | bytes 8 | tf_op jit(solution)/shard_map/psum | solution.py:17
  18.9 3.1 psum.30
  22.0 36.1 %psum.31 = f32[]{:T(128)} all-reduce(f32[]{:T(128)} %psum.30), channel_id=1, replica_groups=mesh['side'=2,'dp_0'=2,'dp_1'=4,'dp_2'=2,'grp'=16] {'grp'}, use_global_device_ids=true, to_apply=%region_4.0 | all-reduce | flops 1 | bytes 8 | tf_op jit(solution)/shard_map/psum | solution.py:17
  63.9 6.7 %all-to-all-start = ((bf16[2,128,2048]{1,0,2:T(2,128)(2,1)}), bf16[2,128,2048]{1,0,2:T(2,128)(2,1)S(1)}, u32[]{:S(2)}, u32[]{:S(2)}) async-start(bf16[2,128,2048]{1,0,2:T(2,128)(2,1)} %copy.157), calls=%async_computation | async-start | bytes 2097152 | tf_op jit(solution)/shard_map/all_to_all | solution.py:175
  72.0 41.6 %all-to-all-done = bf16[2,128,2048]{1,0,2:T(2,128)(2,1)S(1)} async-done(((bf16[2,128,2048]{1,0,2:T(2,128)(2,1)}), bf16[2,128,2048]{1,0,2:T(2,128)(2,1)S(1)}, u32[]{:S(2)}, u32[]{:S(2)}) %all-to-all-start) | async-done | bytes 1048608 | tf_op jit(solution)/shard_map/all_to_all | solution.py:175
  115.4 4.2 %collective-permute-start = (bf16[2,2048,128]{2,1,0:T(8,128)(2,1)S(1)}, bf16[2,2048,128]{2,1,0:T(8,128)(2,1)S(1)}, u32[]{:S(2)}, u32[]{:S(2)}) collective-permute-start(bf16[2,2048,128]{2,1,0:T(8,128)(2,1)S(1)} %copy.159), channel_id=1, source_target_pairs={{0,256},{256,0},{1,257},{257,1},{2,258},{258,2},{3,259},{259,3},{4... | collective-permute-start | bytes 3145736 | tf_op jit(solution)/shard_map/ppermute | solution.py:28
  120.7 18.2 %collective-permute-done = bf16[2,2048,128]{2,1,0:T(8,128)(2,1)S(1)} collective-permute-done((bf16[2,2048,128]{2,1,0:T(8,128)(2,1)S(1)}, bf16[2,2048,128]{2,1,0:T(8,128)(2,1)S(1)}, u32[]{:S(2)}, u32[]{:S(2)}) %collective-permute-start) | collective-permute-done | bytes 1048608 | tf_op jit(solution)/shard_map/ppermute | solution.py:28
  138.8 176.5 %conditional.1 = (bf16[2,2048,128]{1,2,0:T(8,128)(2,1)S(1)}) conditional(s32[]{:T(128)} %convert_element_type.93, (bf16[2,2048,128]{1,2,0:T(8,128)(2,1)S(1)}, s32[16]{0:T(128)S(1)}, s32[16,5]{1,0:T(8,128)S(1)}, s32[16,5,8]{0,2,1:T(8,128)S(1)}, s32[16]{0:T(128)S(1)}, /*index=5*/bf16[2,2048,128]{2,1,0:T(8,128)(2,1)S(1)}, ...), branch_computations={%region_12.23_spmd, %region_21.29_spmd} | conditional | flops 520039488 | bytes 74372872 | solution.py:206
  146.0 61.5 %while.33 = (s32[]{:T(128)}, f32[4,4,2,128]{3,2,1,0:T(2,128)S(1)}, f32[4,4,2,128]{3,2,1,0:T(2,128)S(1)}, s32[4]{0:T(128)S(1)}, pred[16,5]{1,0:T(8,128)(4,1)S(1)}...) while((s32[]{:T(128)}, f32[4,4,2,128]{3,2,1,0:T(2,128)S(1)}, ...), condition=%wide.region_18.19_spmd, body=%wide.region_14.18_spmd.sunk | while | flops 175963328 | bytes 17891416 | solution.py:99
  154.6 2.1 fusion.107
  159.0 2.3 fusion.108
  170.0 2.1 fusion.107
  174.3 2.3 fusion.108
  185.4 2.1 fusion.107
  189.7 2.3 fusion.108
  205.1 2.3 fusion.108
  207.5 2.1 copy.136
  215.3 96.8 %while.34 = (s32[]{:T(128)}, bf16[4,4,128,2,64]{2,1,0,4,3:T(4,128)(2,1)}, bf16[4,4,128,2,64]{2,1,0,4,3:T(4,128)(2,1)}, s32[4]{0:T(128)S(1)}, s32[16,5]{1,0:T(8,1...) while((s32[]{:T(128)}, ...), condition=%wide.region_20.22_spmd, body=%wide.region_19.21_spmd.sunk | while | flops 343551168 | bytes 33408092 | solution.py:157
  222.7 2.1 fusion.116
  231.6 4.3 %fusion.118 = bf16[1,4,128,2,64]{2,4,3,1,0:T(8,128)(2,1)S(1)} fusion(bf16[4,640,2,64]{1,3,2,0:T(8,128)(2,1)S(1)} %copy.279, f32[4,2,640,128]{3,2,1,0:T(8,128)} %fusion.116, bf16[4,640,2,64]{1,3,2,0:T(8,128)(2,1)} %copy.278, f32[4,2,640]{2,1,0:T(2,128)} %bitcast.235, f32[4,2,640]{2,1,0:T(2,128)} %bitcast.233, pred[4,640]{1,0:T(4,128)(4,1)} %bitcast.241, ...), kind=kOutput, calls=%fused_computation.51.clone.1 | convolution fusion | flops 172425216 | bytes 4237824 | tf_op jit(solution)/shard_map/cond/branch_0_fun/while/body/eval_jaxpr/ghqk,gqhd->gkhd/dot_general | solution.py:152
  236.0 2.5 fusion.117
  247.0 2.1 fusion.116
  255.8 4.3 %fusion.118 = bf16[1,4,128,2,64]{2,4,3,1,0:T(8,128)(2,1)S(1)} fusion(bf16[4,640,2,64]{1,3,2,0:T(8,128)(2,1)S(1)} %copy.279, f32[4,2,640,128]{3,2,1,0:T(8,128)} %fusion.116, bf16[4,640,2,64]{1,3,2,0:T(8,128)(2,1)} %copy.278, f32[4,2,640]{2,1,0:T(2,128)} %bitcast.235, f32[4,2,640]{2,1,0:T(2,128)} %bitcast.233, pred[4,640]{1,0:T(4,128)(4,1)} %bitcast.241, ...), kind=kOutput, calls=%fused_computation.51.clone.1 | convolution fusion | flops 172425216 | bytes 4237824 | tf_op jit(solution)/shard_map/cond/branch_0_fun/while/body/eval_jaxpr/ghqk,gqhd->gkhd/dot_general | solution.py:152
  260.2 2.5 fusion.117
  271.2 2.1 fusion.116
  280.0 4.3 %fusion.118 = bf16[1,4,128,2,64]{2,4,3,1,0:T(8,128)(2,1)S(1)} fusion(bf16[4,640,2,64]{1,3,2,0:T(8,128)(2,1)S(1)} %copy.279, f32[4,2,640,128]{3,2,1,0:T(8,128)} %fusion.116, bf16[4,640,2,64]{1,3,2,0:T(8,128)(2,1)} %copy.278, f32[4,2,640]{2,1,0:T(2,128)} %bitcast.235, f32[4,2,640]{2,1,0:T(2,128)} %bitcast.233, pred[4,640]{1,0:T(4,128)(4,1)} %bitcast.241, ...), kind=kOutput, calls=%fused_computation.51.clone.1 | convolution fusion | flops 172425216 | bytes 4237824 | tf_op jit(solution)/shard_map/cond/branch_0_fun/while/body/eval_jaxpr/ghqk,gqhd->gkhd/dot_general | solution.py:152
  284.4 2.5 fusion.117
  295.4 2.1 fusion.116
  304.2 4.3 %fusion.118 = bf16[1,4,128,2,64]{2,4,3,1,0:T(8,128)(2,1)S(1)} fusion(bf16[4,640,2,64]{1,3,2,0:T(8,128)(2,1)S(1)} %copy.279, f32[4,2,640,128]{3,2,1,0:T(8,128)} %fusion.116, bf16[4,640,2,64]{1,3,2,0:T(8,128)(2,1)} %copy.278, f32[4,2,640]{2,1,0:T(2,128)} %bitcast.235, f32[4,2,640]{2,1,0:T(2,128)} %bitcast.233, pred[4,640]{1,0:T(4,128)(4,1)} %bitcast.241, ...), kind=kOutput, calls=%fused_computation.51.clone.1 | convolution fusion | flops 172425216 | bytes 4237824 | tf_op jit(solution)/shard_map/cond/branch_0_fun/while/body/eval_jaxpr/ghqk,gqhd->gkhd/dot_general | solution.py:152
  308.6 2.5 fusion.117
  316.1 59.1 %all_to_all.33 = bf16[2,2048,128]{2,0,1:T(2,128)(2,1)S(1)} all-to-all(bf16[2,2048,128]{2,0,1:T(2,128)(2,1)S(1)} %copy.164), channel_id=1, replica_groups=mesh['side'=2,'dp_0'=2,'dp_1'=4,'dp_2'=2,'grp'=16] {'grp'}, dimensions={1} | all-to-all | bytes 2097152 | tf_op jit(solution)/shard_map/all_to_all | solution.py:207
  (276 shorter events, 129.6 us)
Async XLA Ops:
  61.9 8.8 %copy-start.7 = (s32[1,8]{1,0:T(1,128)S(1)}, s32[1,8]{1,0:T(1,128)}, u32[]{:S(2)}) copy-start(s32[1,8]{1,0:T(1,128)} %param.19) | copy-start | bytes 100
  61.9 8.9 %copy-start.6 = (s32[1,8]{1,0:T(1,128)S(1)}, s32[1,8]{1,0:T(1,128)}, u32[]{:S(2)}) copy-start(s32[1,8]{1,0:T(1,128)} %param.18) | copy-start | bytes 100
  63.9 49.6 %all-to-all-start = ((bf16[2,128,2048]{1,0,2:T(2,128)(2,1)}), bf16[2,128,2048]{1,0,2:T(2,128)(2,1)S(1)}, u32[]{:S(2)}, u32[]{:S(2)}) async-start(bf16[2,128,2048]{1,0,2:T(2,128)(2,1)} %copy.157), calls=%async_computation | async-start | bytes 2097152 | tf_op jit(solution)/shard_map/all_to_all | solution.py:175
  115.4 23.4 %collective-permute-start = (bf16[2,2048,128]{2,1,0:T(8,128)(2,1)S(1)}, bf16[2,2048,128]{2,1,0:T(8,128)(2,1)S(1)}, u32[]{:S(2)}, u32[]{:S(2)}) collective-permute-start(bf16[2,2048,128]{2,1,0:T(8,128)(2,1)S(1)} %copy.159), channel_id=1, source_target_pairs={{0,256},{256,0},{1,257},{257,1},{2,258},{258,2},{3,259},{259,3},{4... | collective-permute-start | bytes 3145736 | tf_op jit(solution)/shard_map/ppermute | solution.py:28
  207.5 6.1 %copy-start.1 = (bf16[16,8,16,128]{3,1,2,0:T(8,128)(2,1)S(1)}, bf16[16,8,16,128]{3,1,2,0:T(8,128)(2,1)}, u32[]{:S(2)}) copy-start(bf16[16,8,16,128]{3,1,2,0:T(8,128)(2,1)} %get-tuple-element.475) | copy-start | bytes 1572868 | tf_op jit(solution)/shard_map/cond
  215.3 3.1 copy-start.4
  215.3 12.6 %copy-start.2 = (f32[16,2,128]{2,1,0:T(2,128)}, f32[16,2,128]{2,1,0:T(2,128)S(1)}, u32[]{:S(2)}) copy-start(f32[16,2,128]{2,1,0:T(2,128)S(1)} %get-tuple-element.849) | copy-start | bytes 49156 | tf_op jit(solution)/shard_map/cond/branch_0_fun/while
  231.6 4.4 %copy-start = (f32[4,2,640,128]{3,2,1,0:T(8,128)S(1)}, f32[4,2,640,128]{3,2,1,0:T(8,128)}, u32[]{:S(2)}) copy-start(f32[4,2,640,128]{3,2,1,0:T(8,128)} %fusion.116) | copy-start | bytes 7864324 | tf_op jit(solution)/shard_map/cond/branch_0_fun/while
  235.9 3.5 copy-start.3
  235.9 3.5 copy-start.5
  235.9 3.5 copy-start.9
  239.5 1.3 copy-start.8
  239.5 3.1 copy-start.4
  239.5 12.6 %copy-start.2 = (f32[16,2,128]{2,1,0:T(2,128)}, f32[16,2,128]{2,1,0:T(2,128)S(1)}, u32[]{:S(2)}) copy-start(f32[16,2,128]{2,1,0:T(2,128)S(1)} %get-tuple-element.849) | copy-start | bytes 49156 | tf_op jit(solution)/shard_map/cond/branch_0_fun/while
  255.8 4.4 %copy-start = (f32[4,2,640,128]{3,2,1,0:T(8,128)S(1)}, f32[4,2,640,128]{3,2,1,0:T(8,128)}, u32[]{:S(2)}) copy-start(f32[4,2,640,128]{3,2,1,0:T(8,128)} %fusion.116) | copy-start | bytes 7864324 | tf_op jit(solution)/shard_map/cond/branch_0_fun/while
  260.1 3.5 copy-start.3
  260.2 3.5 copy-start.5
  260.2 3.5 copy-start.9
  263.7 1.3 copy-start.8
  263.7 3.1 copy-start.4
  263.7 12.6 %copy-start.2 = (f32[16,2,128]{2,1,0:T(2,128)}, f32[16,2,128]{2,1,0:T(2,128)S(1)}, u32[]{:S(2)}) copy-start(f32[16,2,128]{2,1,0:T(2,128)S(1)} %get-tuple-element.849) | copy-start | bytes 49156 | tf_op jit(solution)/shard_map/cond/branch_0_fun/while
  280.0 4.4 %copy-start = (f32[4,2,640,128]{3,2,1,0:T(8,128)S(1)}, f32[4,2,640,128]{3,2,1,0:T(8,128)}, u32[]{:S(2)}) copy-start(f32[4,2,640,128]{3,2,1,0:T(8,128)} %fusion.116) | copy-start | bytes 7864324 | tf_op jit(solution)/shard_map/cond/branch_0_fun/while
  284.3 3.6 copy-start.3
  284.4 3.6 copy-start.5
  284.4 3.5 copy-start.9
  287.9 1.3 copy-start.8
  287.9 3.1 copy-start.4
  287.9 12.6 %copy-start.2 = (f32[16,2,128]{2,1,0:T(2,128)}, f32[16,2,128]{2,1,0:T(2,128)S(1)}, u32[]{:S(2)}) copy-start(f32[16,2,128]{2,1,0:T(2,128)S(1)} %get-tuple-element.849) | copy-start | bytes 49156 | tf_op jit(solution)/shard_map/cond/branch_0_fun/while
  304.2 4.4 %copy-start = (f32[4,2,640,128]{3,2,1,0:T(8,128)S(1)}, f32[4,2,640,128]{3,2,1,0:T(8,128)}, u32[]{:S(2)}) copy-start(f32[4,2,640,128]{3,2,1,0:T(8,128)} %fusion.116) | copy-start | bytes 7864324 | tf_op jit(solution)/shard_map/cond/branch_0_fun/while
  308.6 3.5 copy-start.3
  308.6 3.5 copy-start.5
  308.6 3.5 copy-start.9
  (1 other events, 1.3 us)
where the time goes:
time: 380 us; the launch traced here: 377 us
  local copies, waits for them, and re-layouts  117 us (31%)
  blocking collectives  116 us (31%)
  waiting for transfers between devices  59.7 us (16%)
  matrix products  53.4 us (14%)
  other arithmetic  12.4 us (3%)
  starting transfers between devices  10.9 us (3%)
  loops' own time  6.69 us (2%)
    all_to_all x1, blocking collectives, per_device(): lax.all_to_all(final, 'grp', split_axis=1, concat_axis=2, tiled=True)  59.1 us
    psum x4, blocking collectives, over_axes(): value = lax.psum(value, axis)  56.8 us
    all_to_all x1, waiting for transfers between devices, per_device(): lax.all_to_all(prepared, 'grp', split_axis=2, concat_axis=1, tiled=True)  41.6 us
    ppermute x1, waiting for transfers between devices, partner_2(): return lax.ppermute(block, axis, route)  18.2 us
    dot_general x4, matrix products, key_one_group(): jnp.einsum('ghqk,gqhd->gkhd', dscores, query_window, preferred_element_ty...  17.3 us
    dot_general x4, matrix products, key_one_group(): jnp.einsum('ghqk,gqhd->gkhd', probs_b, cot_window, preferred_element_type...  10.2 us
    reshape x8, local copies, waits for them, and re-layouts, key_one_group(): jnp.take(cot_blocks, picked, axis=0).reshape(4, window_rows, head_count, HD)  9.82 us
    dot_general x4, matrix products, query_one_group(): jnp.einsum('ghqk,gkhd->gqhd', probs_b, value_window, preferred_element_ty...  9.29 us
  transfers between devices with their start and end apart: 2, of which 2 were waited for; matrix products, arithmetic and copies ran while one was open for 1% of the time, Pallas kernels for 0%

commit v1 on v0

v1 whole, which is shorter than its diff:
```python
import functools
import math

import jax
import jax.numpy as jnp
from jax import lax
from jax.experimental import pallas as pl
from jax.experimental.pallas import tpu as pltpu
from jax.sharding import Mesh
from jax.sharding import PartitionSpec as P

HD = 64
BLOCK = 128
MOST = 5
LANES = 2 * HD
DP_GRP = ("dp_0", "dp_1", "dp_2", "grp")
DP = ("dp_0", "dp_1", "dp_2")
HEADS = ("side", "grp")
EXP2_SCALE = math.log2(math.e) / math.sqrt(HD)


def over_axes(value, axes):
    for axis in axes:
        value = lax.psum(value, axis)
    return value


def low_lanes(shape):
    return lax.broadcasted_iota(jnp.int32, shape, len(shape) - 1) < HD


def pack_kernel(scale_ref, rows_ref, out_ref):
    pair_count = rows_ref.shape[2] // LANES
    scale = jnp.broadcast_to(scale_ref[...], (BLOCK, LANES))
    for pair in range(pair_count):
        cols = slice(pair * LANES, (pair + 1) * LANES)
        first = rows_ref[0, :, cols]
        second = (rows_ref[1, :, cols].astype(jnp.float32) * scale).astype(jnp.bfloat16)
        out_ref[2 * pair] = jnp.concatenate([first[:, :HD], second[:, :HD]], axis=1)
        out_ref[2 * pair + 1] = jnp.concatenate([first[:, HD:], second[:, HD:]], axis=1)


def unpack_kernel(coef_ref, side_ref, heads_ref, out_ref):
    pair_count = out_ref.shape[2] // LANES
    side = side_ref[0]
    coef = jnp.where(low_lanes((BLOCK, LANES)), coef_ref[0], coef_ref[1])
    for pair in range(pair_count):
        cols = slice(pair * LANES, (pair + 1) * LANES)
        one = (heads_ref[2 * pair].astype(jnp.float32) * coef).astype(jnp.bfloat16)
        two = (heads_ref[2 * pair + 1].astype(jnp.float32) * coef).astype(jnp.bfloat16)
        out_ref[side, :, cols] = jnp.concatenate([one[:, :HD], two[:, :HD]], axis=1)
        out_ref[1 - side, :, cols] = jnp.concatenate([one[:, HD:], two[:, HD:]], axis=1)


def attention_kernel(start_ref, count_ref, rows_ref, out_ref, total_ref):
    token_count = rows_ref.shape[0] // 2
    block_count = token_count // BLOCK
    total_ref[...] = jnp.zeros_like(total_ref)

    def block_with(window, dec_row, enc_row):
        query = rows_ref[pl.ds(dec_row, BLOCK), :]
        low = low_lanes(query.shape)
        zero = jnp.zeros_like(query)
        split = jnp.concatenate(
            [jnp.where(low, query, zero), jnp.where(low, zero, query)], axis=0
        )
        keys = rows_ref[pl.ds(enc_row, window * BLOCK), :]
        both = lax.dot_general(
            keys, split, (((1,), (1,)), ((), ())), preferred_element_type=jnp.float32
        )
        scores = both[:, :BLOCK] * EXP2_SCALE
        dprobs = both[:, BLOCK:]
        raw = jnp.exp2(scores - jnp.max(scores, axis=0, keepdims=True))
        probs = raw * (1.0 / jnp.sum(raw, axis=0, keepdims=True))
        row_dot = jnp.sum(probs * dprobs, axis=0, keepdims=True)
        dscores = probs * (dprobs - row_dot)
        pair = jnp.concatenate(
            [dscores.astype(jnp.bfloat16), probs.astype(jnp.bfloat16)], axis=1
        )
        total_ref[pl.ds(enc_row, window * BLOCK), :] += jnp.dot(
            pair, split, preferred_element_type=jnp.float32
        )
        mixed = lax.dot_general(
            pair, keys, (((0,), (0,)), ((), ())), preferred_element_type=jnp.float32
        )
        out_ref[pl.ds(dec_row, BLOCK), :] = jnp.where(
            low, mixed[:BLOCK], mixed[BLOCK:]
        ).astype(jnp.bfloat16)

    def step(block, carry):
        dec_row = pl.multiple_of(token_count + block * BLOCK, BLOCK)
        enc_row = pl.multiple_of(start_ref[block] * BLOCK, BLOCK)
        for window in range(1, MOST + 1):

            @pl.when(count_ref[block] == window)
            def _():
                block_with(window, dec_row, enc_row)

        return carry

    lax.fori_loop(0, block_count, step, 0)
    out_ref[pl.ds(0, token_count), :] = total_ref[...].astype(jnp.bfloat16)


def encoder_ranges(enc_row, dec_row, block_count):
    enc_ends = jnp.cumsum(enc_row)
    dec_ends = jnp.cumsum(dec_row)
    blocks = jnp.arange(block_count, dtype=jnp.int32)
    inside = (blocks[:, None] >= (dec_ends - dec_row)[None, :]) & (
        blocks[:, None] < dec_ends[None, :]
    )
    starts = jnp.sum(jnp.where(inside, (enc_ends - enc_row)[None, :], 0), axis=1)
    counts = jnp.sum(jnp.where(inside, enc_row[None, :], 0), axis=1)
    return starts.astype(jnp.int32), counts.astype(jnp.int32)


VMEM = pl.BlockSpec(memory_space=pltpu.VMEM)
SMEM = pl.BlockSpec(memory_space=pltpu.SMEM)


def per_device(attn_inputs, token_weight, enc_lens, dec_lens):
    local_rows = attn_inputs[0]
    slots, row_count, feature_count = local_rows.shape
    head_count = feature_count // HD
    block_count = head_count // 2
    side = lax.axis_index("side")
    scale = jnp.where(side == 1, token_weight, 1.0)[:, None]
    packed = pl.pallas_call(
        pack_kernel,
        out_shape=jax.ShapeDtypeStruct((head_count, row_count, LANES), jnp.bfloat16),
        in_specs=[VMEM, VMEM],
        out_specs=VMEM,
        name="pack",
    )(scale, local_rows)
    arrived = lax.all_to_all(packed, HEADS, split_axis=0, concat_axis=0, tiled=True)
    starts, counts = encoder_ranges(enc_lens[0], dec_lens[0], lax.axis_size("grp"))
    rows = arrived.reshape(-1, LANES)
    worked = pl.pallas_call(
        attention_kernel,
        out_shape=jax.ShapeDtypeStruct(rows.shape, jnp.bfloat16),
        in_specs=[SMEM, SMEM, VMEM],
        out_specs=VMEM,
        scratch_shapes=[pltpu.VMEM((rows.shape[0] // 2, LANES), jnp.float32)],
        name="attention",
    )(starts, counts, rows)
    returned = lax.all_to_all(
        worked.reshape(arrived.shape), HEADS, split_axis=0, concat_axis=0, tiled=True
    )
    weight_sum = over_axes(jnp.sum(token_weight), DP_GRP)
    factor = row_count * lax.axis_size(DP) * lax.axis_size("grp") / weight_sum
    coef = jnp.stack([factor / math.sqrt(HD), jnp.where(side == 0, factor, 1.0)])
    result = pl.pallas_call(
        unpack_kernel,
        out_shape=jax.ShapeDtypeStruct(local_rows.shape, jnp.bfloat16),
        in_specs=[SMEM, SMEM, VMEM],
        out_specs=VMEM,
        name="unpack",
    )(coef, side.astype(jnp.int32).reshape(1), returned)
    return result[None]


def solution(mesh):
    torus = Mesh(
        mesh.devices.reshape(mesh.shape["side"], 2, 4, 2, mesh.shape["grp"]),
        ("side", "dp_0", "dp_1", "dp_2", "grp"),
    )
    placed = (P("side", None, DP_GRP, None), P(DP_GRP), P(DP, None), P(DP, None))
    return jax.shard_map(
        per_device,
        mesh=torus,
        in_specs=placed,
        out_specs=P("side", None, DP_GRP, None),
        check_vma=False,
    )
```

time: 380 us -> 174 us (0.46)
  the two profiles are of different devices: /device:TPU:8 before, /device:TPU:26 now
where the time goes in v1:
time: 174 us
  blocking collectives  72.1 us (41%)
  waiting for transfers between devices  47.9 us (28%)
  starting transfers between devices  28.5 us (16%)
  Pallas kernels  17.7 us (10%)
  local copies, waits for them, and re-layouts  4.47 us (3%)
  other arithmetic  2.22 us (1%)
    psum x4, blocking collectives, over_axes(): value = lax.psum(value, axis)  72.1 us
    all_to_all x1, waiting for transfers between devices, per_device(): lax.all_to_all(packed, HEADS, split_axis=0, concat_axis=0, tiled=True)  47.9 us
    all_to_all x1, starting transfers between devices, per_device(): lax.all_to_all(packed, HEADS, split_axis=0, concat_axis=0, tiled=True)  18.2 us
    pallas_call x1, Pallas kernels, per_device(): pl.pallas_call(attention_kernel, out_shape=jax.ShapeDtypeStruct(rows.shap...  12.5 us
    all_to_all x1, starting transfers between devices, per_device(): lax.all_to_all(worked.reshape(arrived.shape), HEADS, split_axis=0, concat...  10.3 us
    unnamed x10, local copies, waits for them, and re-layouts  3.74 us
  transfers between devices with their start and end apart: 2, of which 1 were waited for; matrix products, arithmetic and copies ran while one was open for 1% of the time, Pallas kernels for 0%

profile of v1, /device:TPU:26, one launch (start us, length us, event | category | flops | bytes accessed | tf_op | source)
XLA Modules:
  0.0 173.7 jit_solution(981273775400914298)
XLA Ops:
  0.0 0.0 copy-start.3
  0.0 0.7 copy-done.3
  0.7 0.6 fusion.1
  1.3 0.7 copy.6.scale_ref
  2.0 2.6 %pack.1 = bf16[32,128,128]{2,1,0:T(8,128)(2,1)} custom-call(f32[128,1]{1,0:T(8,128)} %copy.6.scale_ref, bf16[2,128,2048]{2,1,0:T(8,128)(2,1)} %bitcast.22), custom_call_target="tpu_custom_call" | custom-call | tf_op jit(solution)/shard_map/pack/pallas_call | solution.py:128
  4.6 18.2 %all-to-all-start = ((bf16[32,128,128]{2,1,0:T(8,128)(2,1)}), bf16[32,128,128]{2,1,0:T(8,128)(2,1)S(1)}, u32[]{:S(2)}, u32[]{:S(2)}) async-start(bf16[32,128,128]{2,1,0:T(8,128)(2,1)} %pack.1), calls=%async_computation | async-start | bytes 2097152 | tf_op jit(solution)/shard_map/all_to_all | solution.py:135
  22.8 0.0 copy-start.4
  22.9 0.6 copy-done.4
  23.5 0.0 copy-start.2
  23.5 0.2 reduce-window.6
  23.7 0.5 copy-done.2
  24.2 0.2 reduce-window_1_clone.1
  24.3 0.7 select_reduce_fusion
  25.0 47.9 %all-to-all-done = bf16[32,128,128]{2,1,0:T(8,128)(2,1)S(1)} async-done(((bf16[32,128,128]{2,1,0:T(8,128)(2,1)}), bf16[32,128,128]{2,1,0:T(8,128)(2,1)S(1)}, u32[]{:S(2)}, u32[]{:S(2)}) %all-to-all-start) | async-done | bytes 1048608 | tf_op jit(solution)/shard_map/all_to_all | solution.py:135
  72.9 0.0 copy-start.1
  72.9 1.0 copy-done.1
  73.9 12.5 %attention.1 = bf16[4096,128]{1,0:T(8,128)(2,1)} custom-call(s32[16]{0:T(128)} %get-tuple-element.6.start_ref, s32[16]{0:T(128)} %get-tuple-element.5.count_ref, bf16[4096,128]{1,0:T(8,128)(2,1)} %bitcast.21), custom_call_target="tpu_custom_call" | custom-call | tf_op jit(solution)/shard_map/attention/pallas_call | solution.py:138
  86.4 10.3 %all-to-all-start.1 = ((bf16[32,128,128]{2,1,0:T(8,128)(2,1)}), bf16[32,128,128]{2,1,0:T(8,128)(2,1)S(1)}, u32[]{:S(2)}, u32[]{:S(2)}) async-start(bf16[32,128,128]{2,1,0:T(8,128)(2,1)} %bitcast.20), calls=%async_computation.1 | async-start | bytes 2097152 | tf_op jit(solution)/shard_map/all_to_all | solution.py:146
  96.7 5.4 %psum.28 = f32[]{:T(128)} all-reduce(f32[]{:T(128)} %get-tuple-element.8), channel_id=1, replica_groups=mesh['side'=2,'dp_0'=2,'dp_1'=4,'dp_2'=2,'grp'=16] {'dp_0'}, use_global_device_ids=true, to_apply=%region_1.2 | all-reduce | flops 1 | bytes 8 | tf_op jit(solution)/shard_map/psum | solution.py:24
  102.2 8.7 %psum.29 = f32[]{:T(128)} all-reduce(f32[]{:T(128)} %psum.28), channel_id=1, replica_groups=mesh['side'=2,'dp_0'=2,'dp_1'=4,'dp_2'=2,'grp'=16] {'dp_1'}, use_global_device_ids=true, to_apply=%region_2.3 | all-reduce | flops 1 | bytes 8 | tf_op jit(solution)/shard_map/psum | solution.py:24
  110.9 3.1 %psum.30 = f32[]{:T(128)} all-reduce(f32[]{:T(128)} %psum.29), channel_id=1, replica_groups=mesh['side'=2,'dp_0'=2,'dp_1'=4,'dp_2'=2,'grp'=16] {'dp_2'}, use_global_device_ids=true, to_apply=%region_3.4 | all-reduce | flops 1 | bytes 8 | tf_op jit(solution)/shard_map/psum | solution.py:24
  113.9 54.9 %psum.31 = f32[]{:T(128)} all-reduce(f32[]{:T(128)} %psum.30), channel_id=1, replica_groups=mesh['side'=2,'dp_0'=2,'dp_1'=4,'dp_2'=2,'grp'=16] {'grp'}, use_global_device_ids=true, to_apply=%region_4.5 | all-reduce | flops 1 | bytes 8 | tf_op jit(solution)/shard_map/psum | solution.py:24
  169.5 0.6 pad_maximum_fusion.coef_ref
  170.1 0.0 all-to-all-done.1.heads_ref
  170.1 0.0 copy-start
  170.1 1.0 copy-done
  171.1 2.6 %unpack.1 = bf16[2,128,2048]{2,1,0:T(8,128)(2,1)} custom-call(f32[2]{0:T(128)} %pad_maximum_fusion.coef_ref, s32[1]{0:T(128)} %bitcast.2.side_ref, bf16[32,128,128]{2,1,0:T(8,128)(2,1)} %copy-done), custom_call_target="tpu_custom_call" | custom-call | tf_op jit(solution)/shard_map/unpack/pallas_call | solution.py:152
  (1 shorter events, 0.0 us)
Async XLA Ops:
  0.0 0.7 copy-start.3
  4.6 68.3 %all-to-all-start = ((bf16[32,128,128]{2,1,0:T(8,128)(2,1)}), bf16[32,128,128]{2,1,0:T(8,128)(2,1)S(1)}, u32[]{:S(2)}, u32[]{:S(2)}) async-start(bf16[32,128,128]{2,1,0:T(8,128)(2,1)} %pack.1), calls=%async_computation | async-start | bytes 2097152 | tf_op jit(solution)/shard_map/all_to_all | solution.py:135
  22.8 0.7 copy-start.4
  23.5 0.7 copy-start.2
  72.9 1.0 copy-start.1
  86.4 83.7 %all-to-all-start.1 = ((bf16[32,128,128]{2,1,0:T(8,128)(2,1)}), bf16[32,128,128]{2,1,0:T(8,128)(2,1)S(1)}, u32[]{:S(2)}, u32[]{:S(2)}) async-start(bf16[32,128,128]{2,1,0:T(8,128)(2,1)} %bitcast.20), calls=%async_computation.1 | async-start | bytes 2097152 | tf_op jit(solution)/shard_map/all_to_all | solution.py:146
  170.1 1.0 copy-start
